TPU v7x, 32 devices: a whole 2x2x4 slice. The times are simulated.
32 devices in a mesh: replica: 8 (over z, core), group: 4 (over y, x).
Axes of the slice: x: 2, y: 2, z: 4, core: 2. Of those that a mesh axis runs over, the one named last changes fastest.
Arguments:
- tokens: bfloat16 [4, 8192, 768], P('group', 'replica'), may hold values from -6 to 6
- cotangent: bfloat16 [4, 8192, 768], P('group', 'replica'), may hold values from -6 to 6
- lengths: int32 [4, 16], P('group'), may hold values from 256 to 768, as said below
- dealing: int32 [4, 16], P('group'), may hold values from 0 to 15, as said below
- offsets: int32 [4, 8, 2], P('group'), may hold values from 0 to 768, as said below
- attn_gain: float32 [768], P('group'), may hold values from 0.1 to 1.9
- qkv_weight: float32 [768, 2304], P('group'), may hold values from -0.21875 to 0.21875
- out_weight: float32 [768, 768], P('group'), may hold values from -0.875 to 0.875
- mlp_gain: float32 [768], P('group'), may hold values from 0.1 to 1.9
- in_weight: float32 [768, 2304], P('group'), may hold values from -0.21875 to 0.21875
- down_weight: float32 [1152, 768], P('group'), may hold values from -0.1875 to 0.1875
Outputs:
- output: bfloat16 [4, 8192, 768], P('group', 'replica')
- input_grad: bfloat16 [4, 8192, 768], P('group', 'replica')
- attn_gain_grad: float32 [768], P('group')
- qkv_grad: float32 [768, 2304], P('group')
- out_grad: float32 [768, 768], P('group')
- mlp_gain_grad: float32 [768], P('group')
- in_grad: float32 [768, 2304], P('group')
- down_grad: float32 [1152, 768], P('group')
Inputs may be any that keep to these rules, and one draw needn't show every extreme that they name: `lengths`: the 16 sequences of a column lie end to end over its 8192 tokens; the two sequences dealt to one replica index hold 1024 tokens together. `dealing`: for each column a permutation of its sequences: entry k is the given-order number of the sequence that is k-th in dealt order; replica index r takes dealt sequences 2 * r to 2 * r + 1. `offsets`: exclusive running sums of the lengths of each replica index's dealt sequences, in dealt order.
All inputs are finite; a program needn't handle non-finite values.
Results may differ from a plain program's by a relative error of at most 0.02.
Values may be sent and summed in bfloat16 or wider, within the bound.
No kernel may reach another device: no remote copies, remote signals or barrier semaphores. Data moves between devices by JAX's collectives and lax.ppermute only.
A program may use at most 256 MiB of HBM per device.

v0:
```python
import math
import jax
import jax.numpy as jnp
from jax import lax
from jax.sharding import PartitionSpec as P

HEADS = 12
HEAD_DIM = 64
epsilon = 1e-05
big_negative = -1e30
rope_base = 160000.0


def column_starts(lengths):
    return jnp.cumsum(lengths) - lengths


def dealt_map(lengths, dealing, offsets, replica_index, tok_rows):
    seq_count = lengths.shape[0]
    per_device = offsets.shape[1]
    starts = column_starts(lengths)
    slot_ids = jnp.arange(tok_rows, dtype=jnp.int32)
    own_starts = lax.dynamic_index_in_dim(offsets, replica_index, 0, keepdims=False)
    segment = jnp.sum((slot_ids[:, None] >= own_starts[None, 1:]).astype(jnp.int32), axis=1)
    choose = segment[:, None] == jnp.arange(per_device, dtype=jnp.int32)[None, :]
    begin_at = jnp.sum(jnp.where(choose, own_starts[None, :], 0), axis=1)
    positions = slot_ids - begin_at
    dealt = replica_index * per_device + segment
    seq_range = jnp.arange(seq_count, dtype=jnp.int32)
    dealt_hits = dealt[:, None] == seq_range[None, :]
    given = jnp.sum(jnp.where(dealt_hits, dealing[None, :], 0), axis=1)
    found_seq = given[:, None] == seq_range[None, :]
    first_at = jnp.sum(jnp.where(found_seq, starts[None, :], 0), axis=1)
    source = jnp.clip(first_at + positions, 0, tok_rows * offsets.shape[0] - 1)
    return (source, segment, positions)


def given_map(lengths, dealing, offsets, column_pos, tok_rows):
    seq_count = lengths.shape[0]
    per_device = offsets.shape[1]
    starts = column_starts(lengths)
    seq_range = jnp.arange(seq_count, dtype=jnp.int32)
    seq_id = jnp.sum((column_pos[:, None] >= starts[None, 1:]).astype(jnp.int32), axis=1)
    found_seq = seq_id[:, None] == seq_range[None, :]
    first_at = jnp.sum(jnp.where(found_seq, starts[None, :], 0), axis=1)
    positions = column_pos - first_at
    matches = dealing[None, :] == seq_id[:, None]
    dealt = jnp.sum(jnp.where(matches, seq_range[None, :], 0), axis=1)
    flat_starts = offsets.reshape(-1)
    dealt_hits = dealt[:, None] == seq_range[None, :]
    begin_at = jnp.sum(jnp.where(dealt_hits, flat_starts[None, :], 0), axis=1)
    target = dealt // per_device * tok_rows + begin_at + positions
    return jnp.clip(target, 0, tok_rows * offsets.shape[0] - 1)


def rotary(values, positions, head_count, head_dim):
    tok_rows = values.shape[0]
    half_dim = head_dim // 2
    frequency = jnp.exp(
        -(jnp.arange(half_dim, dtype=jnp.float32) * (2.0 / head_dim)) * math.log(rope_base)
    )
    angles = positions.astype(jnp.float32)[:, None] * frequency[None, :]
    cosine = jnp.cos(angles)[:, None, :]
    sine_part = jnp.sin(angles)[:, None, :]
    shaped = values.reshape(tok_rows, head_count, head_dim)
    lower_half = shaped[..., :half_dim]
    upper_half = shaped[..., half_dim:]
    turned = jnp.concatenate(
        [
            lower_half * cosine - upper_half * sine_part,
            upper_half * cosine + lower_half * sine_part,
        ],
        axis=-1,
    )
    return turned.reshape(tok_rows, head_count * head_dim)


def layer_norm(values, gain_vec):
    row_mean = jnp.mean(values, axis=-1, keepdims=True)
    centred = values - row_mean
    spread = jnp.mean(centred * centred, axis=-1, keepdims=True)
    return centred * lax.rsqrt(spread + epsilon) * gain_vec


def geglu(lifted):
    hidden_width = lifted.shape[1] // 2
    return jax.nn.gelu(lifted[:, :hidden_width], approximate=False) * lifted[:, hidden_width:]


def pick_rows(index_map, carry, piece):
    piece_rows = piece.shape[1]
    inside = (index_map >= 0) & (index_map < piece_rows)
    taken = jnp.take(piece[0], jnp.clip(index_map, 0, piece_rows - 1), axis=0)
    return jnp.where(inside[:, None], taken, carry)


def soft_block(queries, seg_query, key_heads, segment, score_scale):
    scores = (
        jnp.einsum("qhd,khd->hqk", queries, key_heads, preferred_element_type=jnp.float32)
        * score_scale
    )
    same_seq = seg_query[:, None] == segment[None, :]
    return jnp.where(same_seq[None], scores, big_negative)


def on_device(
    tokens,
    cotangent,
    lengths,
    dealing,
    offsets,
    attn_gain,
    qkv_weight,
    out_weight,
    mlp_gain,
    in_weight,
    down_weight,
):
    tok_rows = tokens.shape[1]
    model_width = tokens.shape[2]
    head_count = HEADS
    head_dim = HEAD_DIM
    score_scale = head_dim ** (-0.5)
    replica_index = lax.axis_index("replica")
    source, segment, positions = dealt_map(
        lengths[0], dealing[0], offsets[0], replica_index, tok_rows
    )
    target = given_map(
        lengths[0],
        dealing[0],
        offsets[0],
        replica_index * tok_rows + jnp.arange(tok_rows, dtype=jnp.int32),
        tok_rows,
    )
    masters = (
        attn_gain.astype(jnp.bfloat16),
        qkv_weight.astype(jnp.bfloat16),
        out_weight.astype(jnp.bfloat16),
        mlp_gain.astype(jnp.bfloat16),
        in_weight.astype(jnp.bfloat16),
        down_weight.astype(jnp.bfloat16),
    )
    weights = (
        lax.all_gather(masters[0], "group", axis=0, tiled=True),
        lax.all_gather(masters[1], "group", axis=0, tiled=True),
        lax.all_gather(masters[2], "group", axis=0, tiled=True),
        lax.all_gather(masters[3], "group", axis=0, tiled=True),
        lax.all_gather(masters[4], "group", axis=0, tiled=True),
        lax.all_gather(masters[5], "group", axis=0, tiled=True),
    )
    blank = jnp.zeros((tok_rows, model_width), jnp.bfloat16)
    dealt_x = pick_rows(source, blank, lax.all_gather(tokens, "replica", axis=1, tiled=True))
    gain_one, w_qkv, w_out, gain_two, w_in, w_down = weights
    gain_first = gain_one.astype(jnp.float32)
    gain_second = gain_two.astype(jnp.float32)
    rows_in = dealt_x.astype(jnp.float32)
    normed = layer_norm(rows_in, gain_first).astype(jnp.bfloat16)
    mixed_proj = jnp.dot(normed, w_qkv, preferred_element_type=jnp.float32)
    queries = (
        rotary(mixed_proj[:, :model_width], positions, head_count, head_dim)
        .astype(jnp.bfloat16)
        .reshape(tok_rows, head_count, head_dim)
    )
    key_heads = (
        rotary(mixed_proj[:, model_width : 2 * model_width], positions, head_count, head_dim)
        .astype(jnp.bfloat16)
        .reshape(tok_rows, head_count, head_dim)
    )
    value_heads = (
        mixed_proj[:, 2 * model_width :]
        .astype(jnp.bfloat16)
        .reshape(tok_rows, head_count, head_dim)
    )
    block_rows = min(512, tok_rows)
    block_count = tok_rows // block_rows
    attended_parts = []
    kept_tops = []
    kept_totals = []
    for number in range(block_count):
        lower_row = number * block_rows
        masked = soft_block(
            queries[lower_row : lower_row + block_rows],
            segment[lower_row : lower_row + block_rows],
            key_heads,
            segment,
            score_scale,
        )
        row_top = jnp.max(masked, axis=-1, keepdims=True)
        exponent = jnp.exp(masked - row_top)
        row_total = jnp.sum(exponent, axis=-1, keepdims=True)
        weights_soft = (exponent / row_total).astype(jnp.bfloat16)
        attended_block = jnp.einsum(
            "hqk,khd->qhd", weights_soft, value_heads, preferred_element_type=jnp.float32
        )
        attended_parts.append(attended_block.astype(jnp.bfloat16))
        kept_tops.append(row_top)
        kept_totals.append(row_total)
    attended = jnp.concatenate(attended_parts, axis=0).reshape(tok_rows, model_width)
    middle = rows_in + jnp.dot(attended, w_out, preferred_element_type=jnp.float32)
    normed_two = layer_norm(middle, gain_second).astype(jnp.bfloat16)
    lifted = jnp.dot(normed_two, w_in, preferred_element_type=jnp.float32)
    hidden = geglu(lifted).astype(jnp.bfloat16)
    output_dealt = (middle + jnp.dot(hidden, w_down, preferred_element_type=jnp.float32)).astype(
        jnp.bfloat16
    )
    output_given = pick_rows(
        target, blank, lax.all_gather(output_dealt[None], "replica", axis=1, tiled=True)
    )
    dealt_dy = pick_rows(source, blank, lax.all_gather(cotangent, "replica", axis=1, tiled=True))
    weights = (
        lax.all_gather(masters[0], "group", axis=0, tiled=True),
        lax.all_gather(masters[1], "group", axis=0, tiled=True),
        lax.all_gather(masters[2], "group", axis=0, tiled=True),
        lax.all_gather(masters[3], "group", axis=0, tiled=True),
        lax.all_gather(masters[4], "group", axis=0, tiled=True),
        lax.all_gather(masters[5], "group", axis=0, tiled=True),
    )
    gain_one, w_qkv, w_out, gain_two, w_in, w_down = weights
    grad_out = dealt_dy.astype(jnp.float32)
    down_partial = jnp.einsum("tf,td->fd", hidden, dealt_dy, preferred_element_type=jnp.float32)
    grad_hidden = jnp.einsum("td,fd->tf", dealt_dy, w_down, preferred_element_type=jnp.float32)
    _, geglu_back = jax.vjp(geglu, lifted)
    grad_lifted = geglu_back(grad_hidden)[0].astype(jnp.bfloat16)
    in_partial = jnp.einsum(
        "td,tf->df", normed_two, grad_lifted, preferred_element_type=jnp.float32
    )
    grad_normed_two = jnp.einsum("tf,df->td", grad_lifted, w_in, preferred_element_type=jnp.float32)
    _, norm_back_two = jax.vjp(layer_norm, middle, gain_second)
    grad_middle_part, gain_two_partial = norm_back_two(grad_normed_two)
    grad_middle = grad_out + grad_middle_part
    grad_branch = grad_middle.astype(jnp.bfloat16)
    out_partial = jnp.einsum("ti,to->io", attended, grad_branch, preferred_element_type=jnp.float32)
    grad_attended = (
        jnp.einsum("to,io->ti", grad_branch, w_out, preferred_element_type=jnp.float32)
        .astype(jnp.bfloat16)
        .reshape(tok_rows, head_count, head_dim)
    )
    grad_keys = jnp.zeros((tok_rows, head_count, head_dim), jnp.float32)
    grad_values = jnp.zeros((tok_rows, head_count, head_dim), jnp.float32)
    grad_query_parts = []
    for number in range(block_count):
        lower_row = number * block_rows
        query_block = queries[lower_row : lower_row + block_rows]
        masked = soft_block(
            query_block,
            segment[lower_row : lower_row + block_rows],
            key_heads,
            segment,
            score_scale,
        )
        weights_full = jnp.exp(masked - kept_tops[number]) / kept_totals[number]
        weights_soft = weights_full.astype(jnp.bfloat16)
        grad_block = grad_attended[lower_row : lower_row + block_rows]
        grad_probs = jnp.einsum(
            "qhd,khd->hqk", grad_block, value_heads, preferred_element_type=jnp.float32
        )
        inner = jnp.sum(weights_full * grad_probs, axis=-1, keepdims=True)
        grad_scores = (weights_full * (grad_probs - inner)).astype(jnp.bfloat16)
        grad_query_parts.append(
            jnp.einsum("hqk,khd->qhd", grad_scores, key_heads, preferred_element_type=jnp.float32)
            * score_scale
        )
        grad_keys = (
            grad_keys
            + jnp.einsum(
                "hqk,qhd->khd", grad_scores, query_block, preferred_element_type=jnp.float32
            )
            * score_scale
        )
        grad_values = grad_values + jnp.einsum(
            "hqk,qhd->khd", weights_soft, grad_block, preferred_element_type=jnp.float32
        )
    grad_queries = jnp.concatenate(grad_query_parts, axis=0).reshape(tok_rows, model_width)

    def turn_rows(values):
        return rotary(values, positions, head_count, head_dim)

    _, rope_back = jax.vjp(turn_rows, mixed_proj[:, :model_width])
    grad_mixed = jnp.concatenate(
        [
            rope_back(grad_queries)[0],
            rope_back(grad_keys.reshape(tok_rows, model_width))[0],
            grad_values.reshape(tok_rows, model_width),
        ],
        axis=1,
    ).astype(jnp.bfloat16)
    qkv_partial = jnp.einsum("td,te->de", normed, grad_mixed, preferred_element_type=jnp.float32)
    grad_normed = jnp.einsum("te,de->td", grad_mixed, w_qkv, preferred_element_type=jnp.float32)
    _, norm_back_one = jax.vjp(layer_norm, rows_in, gain_first)
    grad_rows_part, gain_one_partial = norm_back_one(grad_normed)
    grad_input = (grad_middle + grad_rows_part).astype(jnp.bfloat16)
    grad_given = pick_rows(
        target, blank, lax.all_gather(grad_input[None], "replica", axis=1, tiled=True)
    )
    partial_grads = (
        gain_one_partial,
        qkv_partial,
        out_partial,
        gain_two_partial,
        in_partial,
        down_partial,
    )
    shards = (
        lax.psum_scatter(
            partial_grads[0].astype(jnp.bfloat16), "group", scatter_dimension=0, tiled=True
        ).astype(jnp.float32),
        lax.psum_scatter(
            partial_grads[1].astype(jnp.bfloat16), "group", scatter_dimension=0, tiled=True
        ).astype(jnp.float32),
        lax.psum_scatter(
            partial_grads[2].astype(jnp.bfloat16), "group", scatter_dimension=0, tiled=True
        ).astype(jnp.float32),
        lax.psum_scatter(
            partial_grads[3].astype(jnp.bfloat16), "group", scatter_dimension=0, tiled=True
        ).astype(jnp.float32),
        lax.psum_scatter(
            partial_grads[4].astype(jnp.bfloat16), "group", scatter_dimension=0, tiled=True
        ).astype(jnp.float32),
        lax.psum_scatter(
            partial_grads[5].astype(jnp.bfloat16), "group", scatter_dimension=0, tiled=True
        ).astype(jnp.float32),
    )
    summed = (
        lax.psum(shards[0].astype(jnp.bfloat16), "replica").astype(jnp.float32),
        lax.psum(shards[1].astype(jnp.bfloat16), "replica").astype(jnp.float32),
        lax.psum(shards[2].astype(jnp.bfloat16), "replica").astype(jnp.float32),
        lax.psum(shards[3].astype(jnp.bfloat16), "replica").astype(jnp.float32),
        lax.psum(shards[4].astype(jnp.bfloat16), "replica").astype(jnp.float32),
        lax.psum(shards[5].astype(jnp.bfloat16), "replica").astype(jnp.float32),
    )
    return (
        output_given[None],
        grad_given[None],
        summed[0],
        summed[1],
        summed[2],
        summed[3],
        summed[4],
        summed[5],
    )


def solution(mesh):
    return jax.shard_map(
        on_device,
        mesh=mesh,
        in_specs=(
            P("group", "replica", None),
            P("group", "replica", None),
            P("group", None),
            P("group", None),
            P("group", None, None),
            P("group"),
            P("group", None),
            P("group", None),
            P("group"),
            P("group", None),
            P("group", None),
        ),
        out_specs=(
            P("group", "replica", None),
            P("group", "replica", None),
            P("group"),
            P("group", None),
            P("group", None),
            P("group"),
            P("group", None),
            P("group", None),
        ),
        check_vma=False,
    )
```

profile of v0, /device:TPU:0, one launch (start us, length us, event | category | flops | bytes accessed | tf_op | source)
XLA Modules:
  0.0 1018.6 jit_solution(18329896838933659207)
XLA Ops:
  21.5 11.4 %all-reduce.13 = (bf16[768]{0:T(1024)(128)(2,1)S(1)}, bf16[768]{0:T(1024)(128)(2,1)S(1)}) all-reduce(bf16[768]{0:T(1024)(128)(2,1)S(1)} %dynamic-update-slice, bf16[768]{0:T(1024)(128)(2,1)S(1)} %dynamic-update-slice.1), channel_id=1, replica_groups=mesh['replica'=8,'group'=4] {'group'}, use_global_device_ids=true, to_apply=%add.6 | all-reduce | flops 1536 | bytes 6144
  35.0 94.1 %all-gather.11.cloned.1.call-done = bf16[1,8192,768]{2,1,0:T(8,128)(2,1)} async-done(((bf16[1,1024,768]{2,1,0:T(8,128)(2,1)}), bf16[1,8192,768]{2,1,0:T(8,128)(2,1)}) %all-gather.11.cloned.1.call-update) | async-done | bytes 12582928 | tf_op jit(solution)/shard_map/all_gather | solution.py:152
  141.7 35.2 %all-gather.13.cloned.1.call-done = bf16[768,2304]{1,0:T(8,128)(2,1)} async-done(((bf16[192,2304]{1,0:T(8,128)(2,1)}), bf16[768,2304]{1,0:T(8,128)(2,1)}) %all-gather.13.cloned.1.call-update) | async-done | bytes 3538960 | tf_op jit(solution)/shard_map/all_gather | solution.py:145
  210.0 14.6 %fusion.109 = (f32[12,512]{1,0:T(8,128)S(1)}, f32[12,512,1024]{2,1,0:T(8,128)}) fusion(pred[512,1024]{1,0:T(8,128)(4,1)} %get-tuple-element.88, bf16[1024,12,32]{0,2,1:T(8,128)(2,1)} %copy-done.17, bf16[1024,12,32]{0,2,1:T(8,128)(2,1)} %copy-done.15, bf16[1024,12,32]{0,2,1:T(8,128)(2,1)S(1)} %get-tuple-element.83, ...), kind=kOutput, calls=%fused_computation.205 | convolution fusion | flops 835191808 | bytes 28860416 | tf_op jit(solution)/shard_map/sub | solution.py:189
  224.6 33.6 %fusion.108 = (f32[12,512]{1,0:T(8,128)S(1)}, f32[12,512,1024]{2,1,0:T(8,128)}) fusion(f32[12,512,1024]{2,1,0:T(8,128)} %fusion.62, pred[512,1024]{1,0:T(8,128)(4,1)} %get-tuple-element.89), kind=kOutput, calls=%fused_computation.204 | output fusion | flops 37749760 | bytes 50880512 | tf_op jit(solution)/shard_map/sub | solution.py:189
  258.2 11.4 %fusion.52 = bf16[512,12,64]{0,2,1:T(8,128)(2,1)} fusion(bf16[1024,12,64]{0,2,1:T(8,128)(2,1)S(1)} %bitcast.72, f32[12,512,1024]{2,1,0:T(8,128)} %get-tuple-element.101, f32[12,512]{1,0:T(8,128)S(1)} %get-tuple-element.100), kind=kOutput, calls=%fused_computation.115 | convolution fusion | flops 818282496 | bytes 27549696 | tf_op jit(solution)/shard_map/hqk,khd->qhd/dot_general | solution.py:192
  269.6 11.6 %fusion.49 = bf16[512,12,64]{0,2,1:T(8,128)(2,1)} fusion(bf16[1024,12,64]{0,2,1:T(8,128)(2,1)S(1)} %bitcast.73, f32[12,512,1024]{2,1,0:T(8,128)} %get-tuple-element.99, f32[12,512]{1,0:T(8,128)S(1)} %get-tuple-element.98), kind=kOutput, calls=%fused_computation.114 | convolution fusion | flops 818282496 | bytes 27549696 | tf_op jit(solution)/shard_map/hqk,khd->qhd/dot_general | solution.py:192
  281.2 14.1 %all-gather.21.cloned.1.call-done = bf16[1,8192,768]{2,1,0:T(8,128)(2,1)} async-done(((bf16[1,1024,768]{2,1,0:T(8,128)(2,1)}), bf16[1,8192,768]{2,1,0:T(8,128)(2,1)}) %all-gather.21.cloned.1.call-update) | async-done | bytes 12582928 | tf_op jit(solution)/shard_map/all_gather | solution.py:209
  295.3 11.8 %gather_fusion.2 = bf16[1024,768]{1,0:T(8,128)(2,1)} fusion(bf16[8192,768]{1,0:T(8,128)(2,1)} %bitcast.68, s32[1024]{0:T(1024)S(1)} %get-tuple-element.93), kind=kCustom, calls=%fused_computation.2.clone | custom fusion | bytes 3149824 | tf_op jit(solution)/shard_map/jit(_take)/gather | solution.py:93
  328.2 44.0 %all-gather.17.cloned.1.call-done = bf16[768,2304]{1,0:T(8,128)(2,1)} async-done(((bf16[192,2304]{1,0:T(8,128)(2,1)}), bf16[768,2304]{1,0:T(8,128)(2,1)}) %all-gather.17.cloned.1.call-update) | async-done | bytes 3538960 | tf_op jit(solution)/shard_map/all_gather | solution.py:148
  382.8 23.6 %all-gather.19.cloned.1.call-done = bf16[1152,768]{1,0:T(8,128)(2,1)} async-done(((bf16[288,768]{1,0:T(8,128)(2,1)}), bf16[1152,768]{1,0:T(8,128)(2,1)}) %all-gather.19.cloned.1.call-update) | async-done | bytes 1769488 | tf_op jit(solution)/shard_map/all_gather | solution.py:149
  406.4 14.5 %fusion.42 = (f32[1024,1152]{1,0:T(8,128)}, f32[1024,1152]{1,0:T(8,128)S(1)}, f32[1024,1152]{1,0:T(8,128)S(1)}) fusion(f32[1024,2304]{1,0:T(8,128)} %fusion.93, bf16[1152,768]{1,0:T(8,128)(2,1)} %all-gather.19.cloned.1.call-done, bf16[1024,768]{0,1:T(8,128)(2,1)S(1)} %copy.75, pred[1024]{0:T(1024)(128)(4,1)S(1)} %get-tuple-element.85, ...), kind=kOutput, calls=%fused_computation.111 | convolution fusion | flops 1890189312 | bytes 22218752 | tf_op jit(solution)/shard_map/td,fd->tf/dot_general | solution.py:221
  450.8 19.3 %multiply_reduce_fusion.1 = (f32[12,512]{1,0:T(8,128)S(1)}, f32[12,512,1024]{2,1,0:T(8,128)}) fusion(f32[12,512,1024]{2,1,0:T(8,128)} %get-tuple-element.101, f32[12,512]{1,0:T(8,128)S(1)} %get-tuple-element.100, bf16[512,12,64]{0,2,1:T(8,128)(2,1)S(1)} %bitcast.82, bf16[1024,12,64]{0,2,1:T(8,128)(2,1)S(1)} %bitcast.74), kind=kOutput, calls=%fused_computation.9 | convolution fusion | flops 824174592 | bytes 52740096 | tf_op jit(solution)/shard_map/qhd,khd->hqk/dot_general | solution.py:254
  470.1 19.1 %multiply_reduce_fusion = (f32[12,512]{1,0:T(8,128)S(1)}, f32[12,512,1024]{2,1,0:T(8,128)}) fusion(f32[12,512,1024]{2,1,0:T(8,128)} %get-tuple-element.99, f32[12,512]{1,0:T(8,128)S(1)} %get-tuple-element.98, bf16[512,12,64]{0,2,1:T(8,128)(2,1)S(1)} %bitcast.84, bf16[1024,12,64]{0,2,1:T(8,128)(2,1)S(1)} %bitcast.75), kind=kOutput, calls=%fused_computation.7 | convolution fusion | flops 824174592 | bytes 52740096 | tf_op jit(solution)/shard_map/qhd,khd->hqk/dot_general | solution.py:254
  489.3 17.0 %multiply_convert_fusion.1 = bf16[12,512,1024]{2,1,0:T(8,128)(2,1)S(1)} fusion(f32[12,512,1024]{2,1,0:T(8,128)} %get-tuple-element.109, f32[12,512]{1,0:T(8,128)S(1)} %get-tuple-element.108, f32[12,512,1024]{2,1,0:T(8,128)} %get-tuple-element.101, f32[12,512]{1,0:T(8,128)S(1)} %get-tuple-element.100), kind=kLoop, calls=%fused_computation.8 | loop fusion | flops 25165824 | bytes 62963712 | tf_op jit(solution)/shard_map/convert_element_type | solution.py:258
  506.4 27.2 %multiply_convert_fusion = bf16[12,512,1024]{2,1,0:T(8,128)(2,1)} fusion(f32[12,512,1024]{2,1,0:T(8,128)} %get-tuple-element.107, f32[12,512]{1,0:T(8,128)S(1)} %get-tuple-element.106, f32[12,512,1024]{2,1,0:T(8,128)} %get-tuple-element.99, f32[12,512]{1,0:T(8,128)S(1)} %get-tuple-element.98), kind=kLoop, calls=%fused_computation.6 | loop fusion | flops 25165824 | bytes 62963712 | tf_op jit(solution)/shard_map/convert_element_type | solution.py:258
  619.6 50.1 %reduce-scatter.5.cloned.1.call-done = bf16[192,2304]{1,0:T(8,128)(2,1)} async-done(((bf16[768,2304]{1,0:T(8,128)(2,1)}), bf16[192,2304]{1,0:T(8,128)(2,1)}) %reduce-scatter.5.cloned.1.call-update) | async-done | bytes 884752 | tf_op jit(solution)/shard_map/reduce_scatter | solution.py:307
  698.9 14.6 %all-reduce.10 = (bf16[192]{0:T(256)(128)(2,1)S(1)}, bf16[192]{0:T(256)(128)(2,1)S(1)}) all-reduce(bf16[192]{0:T(256)(128)(2,1)S(1)} %dynamic-slice.4, bf16[192]{0:T(256)(128)(2,1)S(1)} %dynamic-slice.6), channel_id=1, replica_groups=mesh['replica'=8,'group'=4] {'replica'}, use_global_device_ids=true, to_apply=%region_24.26 | all-reduce | flops 384 | bytes 1536 | tf_op jit(solution)/shard_map/psum | solution.py:324
  714.6 25.9 %all-reduce.16.cloned.1.call-done = (bf16[192,2304]{1,0:T(8,128)(2,1)}, bf16[192,768]{1,0:T(8,128)(2,1)}, bf16[192,2304]{1,0:T(8,128)(2,1)}, bf16[288,768]{1,0:T(8,128)(2,1)}) async-done(((bf16[192,2304]{1,0:T(8,128)(2,1)}, bf16[192,768]{1,0:T(8,128)(2,1)}, bf16[192,2304]{1,0:T(8,128)(2,1)}, bf16[288,768]{1,0:T(8,128)(2,1)}), (bf16[192,2304]{1,0:T(8,128)(2,1)}, bf16[192,768]{1,0:T(8,128)(2,1)}, ...) | async-done | bytes 2506768 | tf_op jit(solution)/shard_map/psum | solution.py:325
  747.2 111.1 %all-gather.23.cloned.1.call-done = bf16[8192,768]{0,1:T(8,128)(2,1)} async-done(((bf16[1024,768]{0,1:T(8,128)(2,1)}), bf16[8192,768]{0,1:T(8,128)(2,1)}) %all-gather.23.cloned.1.call-update) | async-done | bytes 12582928 | tf_op jit(solution)/shard_map/all_gather | solution.py:207
  858.3 16.6 %copy.73 = bf16[8192,768]{1,0:T(8,128)(2,1)} copy(bf16[8192,768]{0,1:T(8,128)(2,1)} %all-gather.23.cloned.1.call-done) | data formatting | bytes 25165824 | tf_op jit(solution)/shard_map/all_gather | solution.py:207
  886.5 88.9 %all-gather.25.cloned.1.call-done = bf16[8192,768]{0,1:T(8,128)(2,1)} async-done(((bf16[1024,768]{0,1:T(8,128)(2,1)}), bf16[8192,768]{0,1:T(8,128)(2,1)}) %all-gather.25.cloned.1.call-update) | async-done | bytes 12582928 | tf_op jit(solution)/shard_map/all_gather | solution.py:293
  975.4 16.7 %copy.76 = bf16[8192,768]{1,0:T(8,128)(2,1)} copy(bf16[8192,768]{0,1:T(8,128)(2,1)} %all-gather.25.cloned.1.call-done) | data formatting | bytes 25165824 | tf_op jit(solution)/shard_map/all_gather | solution.py:293
  992.1 11.8 %gather_fusion.3 = bf16[1024,768]{1,0:T(8,128)(2,1)} fusion(bf16[8192,768]{1,0:T(8,128)(2,1)} %copy.76, s32[1024]{0:T(1024)S(1)} %fusion.75), kind=kCustom, calls=%fused_computation.3.clone | custom fusion | bytes 3149824 | tf_op jit(solution)/shard_map/jit(_take)/gather | solution.py:93
  (269 shorter events, 264.3 us)
Async XLA Ops:
  7.2 121.9 %all-gather.11.cloned.1.call-start = ((), (), s32[]{:S(2)}) async-start(), calls=%async_computation.4 | async-start | bytes 14155776 | tf_op jit(solution)/shard_map/all_gather | solution.py:152
  7.9 169.0 %all-gather.13.cloned.1.call-start = ((), (), s32[]{:S(2)}) async-start(), calls=%async_computation.5 | async-start | bytes 4423680 | tf_op jit(solution)/shard_map/all_gather | solution.py:145
  10.6 284.7 %all-gather.21.cloned.1.call-start = ((), (), s32[]{:S(2)}) async-start(), calls=%async_computation.9 | async-start | bytes 14155776 | tf_op jit(solution)/shard_map/all_gather | solution.py:209
  11.4 311.4 %all-gather.15.cloned.1.call-start = ((), (), s32[]{:S(2)}) async-start(), calls=%async_computation.6 | async-start | bytes 1474560 | tf_op jit(solution)/shard_map/all_gather | solution.py:146
  12.2 360.0 %all-gather.17.cloned.1.call-start = ((), (), s32[]{:S(2)}) async-start(), calls=%async_computation.7 | async-start | bytes 4423680 | tf_op jit(solution)/shard_map/all_gather | solution.py:148
  13.3 393.1 %all-gather.19.cloned.1.call-start = ((), (), s32[]{:S(2)}) async-start(), calls=%async_computation.8 | async-start | bytes 2211840 | tf_op jit(solution)/shard_map/all_gather | solution.py:149
  14.2 594.8 %reduce-scatter.7.cloned.1.call-start = ((), (), s32[]{:S(2)}) async-start(), calls=%async_computation.11 | async-start | bytes 1474560 | tf_op jit(solution)/shard_map/reduce_scatter | solution.py:310
  19.6 420.6 %copy-start.53 = (pred[1024]{0:T(1024)(128)(4,1)}, pred[1024]{0:T(1024)(128)(4,1)S(1)}, u32[]{:S(2)}) copy-start(pred[1024]{0:T(1024)(128)(4,1)S(1)} %get-tuple-element.84) | copy-start | bytes 3076
  19.7 420.6 %copy-start.55 = (pred[1024]{0:T(1024)(128)(4,1)}, pred[1024]{0:T(1024)(128)(4,1)S(1)}, u32[]{:S(2)}) copy-start(pred[1024]{0:T(1024)(128)(4,1)S(1)} %get-tuple-element.85) | copy-start | bytes 3076
  32.8 144.1 %copy-start.43 = (f32[768]{0:T(1024)}, f32[768]{0:T(1024)S(1)}, u32[]{:S(2)}) copy-start(f32[768]{0:T(1024)S(1)} %convert_element_type.173) | copy-start | bytes 9220
  33.4 162.2 %copy-start.29 = (f32[1024,32]{0,1:T(8,128)}, f32[1024,32]{0,1:T(8,128)S(1)}, u32[]{:S(2)}) copy-start(f32[1024,32]{0,1:T(8,128)S(1)} %get-tuple-element.86) | copy-start | bytes 393220
  33.4 162.2 %copy-start.31 = (f32[1024,32]{0,1:T(8,128)}, f32[1024,32]{0,1:T(8,128)S(1)}, u32[]{:S(2)}) copy-start(f32[1024,32]{0,1:T(8,128)S(1)} %get-tuple-element.87) | copy-start | bytes 393220
  140.5 182.2 %copy-start.1 = (bf16[1024,768]{0,1:T(8,128)(2,1)}, bf16[1024,768]{0,1:T(8,128)(2,1)S(1)}, u32[]{:S(2)}) copy-start(bf16[1024,768]{0,1:T(8,128)(2,1)S(1)} %copy.68) | copy-start | bytes 4718596
  141.0 35.9 %copy-start.41 = (f32[1024]{0:T(1024)}, f32[1024]{0:T(1024)S(1)}, u32[]{:S(2)}) copy-start(f32[1024]{0:T(1024)S(1)} %broadcast_multiply_fusion.1) | copy-start | bytes 12292
  141.7 35.2 %copy-start.49 = (f32[1024]{0:T(1024)}, f32[1024]{0:T(1024)S(1)}, u32[]{:S(2)}) copy-start(f32[1024]{0:T(1024)S(1)} %fusion.33) | copy-start | bytes 12292
  141.7 35.2 %copy-start.45 = (f32[1024]{0:T(1024)}, f32[1024]{0:T(1024)S(1)}, u32[]{:S(2)}) copy-start(f32[1024]{0:T(1024)S(1)} %fusion.72) | copy-start | bytes 12292
  224.6 33.6 %copy-start.24 = (bf16[1024,768]{0,1:T(8,128)(2,1)S(1)}, bf16[1024,768]{0,1:T(8,128)(2,1)}, u32[]{:S(2)}) copy-start(bf16[1024,768]{0,1:T(8,128)(2,1)} %copy.69) | copy-start | bytes 4718596
  308.8 97.6 %copy-start.5 = (bf16[1024,768]{0,1:T(8,128)(2,1)}, bf16[1024,768]{0,1:T(8,128)(2,1)S(1)}, u32[]{:S(2)}) copy-start(bf16[1024,768]{0,1:T(8,128)(2,1)S(1)} %copy.75) | copy-start | bytes 4718596
  449.0 160.1 %reduce-scatter.11.cloned.1.call-start = ((), (), s32[]{:S(2)}) async-start(), calls=%async_computation.13 | async-start | bytes 2211840 | tf_op jit(solution)/shard_map/reduce_scatter | solution.py:319
  489.3 130.3 %reduce-scatter.9.cloned.1.call-start = ((), (), s32[]{:S(2)}) async-start(), calls=%async_computation.12 | async-start | bytes 4423680 | tf_op jit(solution)/shard_map/reduce_scatter | solution.py:316
  572.3 97.4 %reduce-scatter.5.cloned.1.call-start = ((), (), s32[]{:S(2)}) async-start(), calls=%async_computation.10 | async-start | bytes 4423680 | tf_op jit(solution)/shard_map/reduce_scatter | solution.py:307
  609.0 131.5 %all-reduce.16.cloned.1.call-start = ((), (), s32[]{:S(2)}) async-start(), calls=%async_computation.16 | async-start | bytes 5013504 | tf_op jit(solution)/shard_map/psum | solution.py:325
  669.7 188.6 %all-gather.23.cloned.1.call-start = ((), (), s32[]{:S(2)}) async-start(), calls=%async_computation.14 | async-start | bytes 14155776 | tf_op jit(solution)/shard_map/all_gather | solution.py:207
  676.4 299.0 %all-gather.25.cloned.1.call-start = ((), (), s32[]{:S(2)}) async-start(), calls=%async_computation.15 | async-start | bytes 14155776 | tf_op jit(solution)/shard_map/all_gather | solution.py:293
  (57 other events, 431.1 us)
Sparse Core Ops, SparseCore 0:
  9.6 119.4 all-gather.10
  131.5 45.3 all-gather.12
  178.5 116.6 all-gather.20
  297.0 25.7 all-gather.14
  325.0 47.1 all-gather.16
  373.9 32.4 all-gather.18
  449.2 28.7 reduce-scatter.6
  489.4 32.4 reduce-scatter.10
  572.4 47.1 reduce-scatter.8
  622.5 47.1 reduce-scatter.4
  672.4 68.0 all-reduce.15
  742.0 116.3 all-gather.22
  860.5 114.8 all-gather.24
where the time goes:
time: 1030 us; the launch traced here: 1020 us
  waiting for transfers between devices  510 us (50%)
  matrix products  222 us (22%)
  other arithmetic  122 us (12%)
  local copies, waits for them, and re-layouts  113 us (11%)
  blocking collectives  34.9 us (3%)
  between operations  16.4 us (2%)
    all_gather x1, waiting for transfers between devices, on_device(): lax.all_gather(output_dealt[None], 'replica', axis=1, tiled=True)  111 us
    all_gather x1, waiting for transfers between devices, on_device(): lax.all_gather(tokens, 'replica', axis=1, tiled=True)  94.1 us
    all_gather x1, waiting for transfers between devices, on_device(): lax.all_gather(grad_input[None], 'replica', axis=1, tiled=True)  88.9 us
    reduce_scatter x1, waiting for transfers between devices, on_device(): lax.psum_scatter(partial_grads[1].astype(jnp.bfloat16), 'group', scatter_...  50.1 us
    gather x8, local copies, waits for them, and re-layouts, pick_rows(): taken = jnp.take(piece[0], jnp.clip(index_map, 0, piece_rows - 1), axis=0)  49.9 us
    convert_element_type x2, other arithmetic, on_device(): grad_scores = (weights_full * (grad_probs - inner)).astype(jnp.bfloat16)  44.2 us
    all_gather x1, waiting for transfers between devices, on_device(): lax.all_gather(masters[4], 'group', axis=0, tiled=True)  44 us
    dot_general x2, matrix products, on_device(): jnp.einsum('qhd,khd->hqk', grad_block, value_heads, preferred_element_typ...  38.4 us
  transfers between devices with their start and end apart: 13, of which 11 were waited for; matrix products, arithmetic and copies ran while one was open for 36% of the time, Pallas kernels for 0%

commit v1 on v0

--- a/solution.py
+++ b/solution.py
@@ -1,3 +1,4 @@
+import functools
 import math
 import jax
 import jax.numpy as jnp
@@ -9,6 +10,33 @@
 epsilon = 1e-05
 big_negative = -1e30
 rope_base = 160000.0
+
+
+def convert_rails_over_axis(page, shard_axis, which_dim):
+    reply = lax.psum(1, axis_name=shard_axis)
+    now, spare, base_arr = (reply, lax.axis_index(shard_axis), page.shape[which_dim])
+    gallery = [(idx, (idx + 1) % now) for idx in range(now)]
+    p_next = jnp.zeros(
+        (*page.shape[:which_dim], now * base_arr, *page.shape[which_dim + 1 :]), page.dtype
+    )
+    p_next = lax.dynamic_update_slice_in_dim(p_next, page, spare * base_arr, axis=which_dim)
+    front = prior = page
+    upper = now // 2
+    rack = [(idx, (idx - 1) % now) for idx in range(now)]
+    for ix in [*range(1, upper + 1)]:
+        front = lax.ppermute(front, shard_axis, perm=gallery)
+        p_next = lax.dynamic_update_slice_in_dim(
+            p_next, front, (spare - ix) % now * base_arr, axis=which_dim
+        )
+        if ix < now - upper:
+            prior = lax.ppermute(prior, axis_name=shard_axis, perm=rack)
+            p_next = lax.dynamic_update_slice_in_dim(
+                p_next, prior, (spare + ix) % now * base_arr, axis=which_dim
+            )
+    return p_next
+
+
+fit_links = functools.partial(convert_rails_over_axis, shard_axis="group", which_dim=0)
 
 
 def column_starts(lengths):
@@ -142,7 +170,7 @@
     )
     weights = (
         lax.all_gather(masters[0], "group", axis=0, tiled=True),
-        lax.all_gather(masters[1], "group", axis=0, tiled=True),
+        fit_links(masters[1]),
         lax.all_gather(masters[2], "group", axis=0, tiled=True),
         lax.all_gather(masters[3], "group", axis=0, tiled=True),
         lax.all_gather(masters[4], "group", axis=0, tiled=True),

time: 1030 us -> 1030 us (level)
  waiting for transfers between devices: 510 us -> 475 us
  other arithmetic: 122 us -> 134 us
  local copies, waits for them, and re-layouts: 113 us -> 125 us
    all_gather x1, waiting for transfers between devices: 94.1 us -> 42.3 us  [on_device(): lax.all_gather(tokens, 'replica', axis=1, tiled=True)]
    ppermute x0 -> x3, waiting for transfers between devices: none -> 18.2 us  [the longest x2 18.2 us: convert_rails_over_axis(): front = lax.ppermute(front, shard_axis, perm=gallery)]
    all_gather x1, waiting for transfers between devices: 14.1 us -> 0.02 us  [on_device(): lax.all_gather(cotangent, 'replica', axis=1, tiled=True)]
    unnamed x146 -> x140, local copies, waits for them, and re-layouts: 16.7 us -> 22.4 us
  transfers between devices with their start and end apart: 13 -> 16, of which waited for: 11 -> 11; matrix products, arithmetic and copies ran while one was open for 36% -> 38% of each run, Pallas kernels for 0% -> 0%
where the time goes in v1:
time: 1030 us; the launch traced here: 1020 us
  waiting for transfers between devices  475 us (46%)
  matrix products  221 us (21%)
  other arithmetic  134 us (13%)
  local copies, waits for them, and re-layouts  125 us (12%)
  blocking collectives  43.7 us (4%)
  between operations  16.6 us (2%)
    all_gather x1, waiting for transfers between devices, on_device(): lax.all_gather(output_dealt[None], 'replica', axis=1, tiled=True)  111 us
    all_gather x1, waiting for transfers between devices, on_device(): lax.all_gather(grad_input[None], 'replica', axis=1, tiled=True)  88.9 us
    gather x8, local copies, waits for them, and re-layouts, pick_rows(): taken = jnp.take(piece[0], jnp.clip(index_map, 0, piece_rows - 1), axis=0)  50.6 us
    reduce_scatter x1, waiting for transfers between devices, on_device(): lax.psum_scatter(partial_grads[1].astype(jnp.bfloat16), 'group', scatter_...  50.3 us
    all_gather x1, waiting for transfers between devices, on_device(): lax.all_gather(masters[4], 'group', axis=0, tiled=True)  44 us
    convert_element_type x2, other arithmetic, on_device(): grad_scores = (weights_full * (grad_probs - inner)).astype(jnp.bfloat16)  43.9 us
    all_gather x1, waiting for transfers between devices, on_device(): lax.all_gather(masters[1], 'group', axis=0, tiled=True)  42.7 us
    all_gather x1, waiting for transfers between devices, on_device(): lax.all_gather(tokens, 'replica', axis=1, tiled=True)  42.3 us
  transfers between devices with their start and end apart: 16, of which 11 were waited for; matrix products, arithmetic and copies ran while one was open for 38% of the time, Pallas kernels for 0%

profile of v1, /device:TPU:0, one launch (start us, length us, event | category | flops | bytes accessed | tf_op | source)
XLA Modules:
  0.0 1019.2 jit_solution(2682324507903221928)
XLA Ops:
  41.1 20.1 %all-reduce.13 = (bf16[768]{0:T(1024)(128)(2,1)}, bf16[768]{0:T(1024)(128)(2,1)}) all-reduce(bf16[768]{0:T(1024)(128)(2,1)} %dynamic-update-slice, bf16[768]{0:T(1024)(128)(2,1)} %dynamic-update-slice.1), channel_id=1, replica_groups=mesh['replica'=8,'group'=4] {'group'}, use_global_device_ids=true, to_apply=%add.6 | all-reduce | flops 1536 | bytes 6144
  68.5 18.2 %collective-permute-done.2 = bf16[192,2304]{1,0:T(8,128)(2,1)S(1)} collective-permute-done((bf16[192,2304]{1,0:T(8,128)(2,1)}, bf16[192,2304]{1,0:T(8,128)(2,1)S(1)}, u32[]{:S(2)}, u32[]{:S(2)}) %collective-permute-start.2) | collective-permute-done | bytes 884768 | tf_op jit(solution)/shard_map/ppermute | solution.py:27
  86.8 42.3 %all-gather.11.cloned.1.call-done = bf16[1,8192,768]{2,1,0:T(8,128)(2,1)} async-done(((bf16[1,1024,768]{2,1,0:T(8,128)(2,1)}), bf16[1,8192,768]{2,1,0:T(8,128)(2,1)}) %all-gather.11.cloned.1.call-update) | async-done | bytes 12582928 | tf_op jit(solution)/shard_map/all_gather | solution.py:180
  129.1 11.4 %gather_fusion = bf16[1024,768]{1,0:T(8,128)(2,1)S(1)} fusion(bf16[8192,768]{1,0:T(8,128)(2,1)} %bitcast.69, s32[1024]{0:T(1024)} %get-tuple-element.95), kind=kCustom, calls=%fused_computation.clone | custom fusion | bytes 3149824 | tf_op jit(solution)/shard_map/jit(_take)/gather | solution.py:121
  176.3 15.1 %fusion.109 = (f32[12,512]{1,0:T(8,128)S(1)}, f32[12,512,1024]{2,1,0:T(8,128)}) fusion(pred[512,1024]{1,0:T(8,128)(4,1)} %get-tuple-element.90, bf16[1024,12,32]{0,2,1:T(8,128)(2,1)} %copy-done.17, bf16[1024,12,32]{0,2,1:T(8,128)(2,1)} %copy-done.15, bf16[1024,12,32]{0,2,1:T(8,128)(2,1)S(1)} %get-tuple-element.85, ...), kind=kOutput, calls=%fused_computation.209 | convolution fusion | flops 835191808 | bytes 28860416 | tf_op jit(solution)/shard_map/sub | solution.py:217
  191.3 33.6 %fusion.108 = (f32[12,512]{1,0:T(8,128)S(1)}, f32[12,512,1024]{2,1,0:T(8,128)}) fusion(f32[12,512,1024]{2,1,0:T(8,128)} %fusion.62, pred[512,1024]{1,0:T(8,128)(4,1)} %get-tuple-element.91), kind=kOutput, calls=%fused_computation.208 | output fusion | flops 37749760 | bytes 50880512 | tf_op jit(solution)/shard_map/sub | solution.py:217
  236.2 11.4 %fusion.49 = bf16[512,12,64]{0,2,1:T(8,128)(2,1)} fusion(bf16[1024,12,64]{0,2,1:T(8,128)(2,1)S(1)} %bitcast.73, f32[12,512,1024]{2,1,0:T(8,128)} %get-tuple-element.101, f32[12,512]{1,0:T(8,128)S(1)} %get-tuple-element.100), kind=kOutput, calls=%fused_computation.114 | convolution fusion | flops 818282496 | bytes 27549696 | tf_op jit(solution)/shard_map/hqk,khd->qhd/dot_general | solution.py:220
  247.7 11.8 %gather_fusion.2 = bf16[1024,768]{1,0:T(8,128)(2,1)} fusion(bf16[8192,768]{1,0:T(8,128)(2,1)} %bitcast.68, s32[1024]{0:T(1024)S(1)} %copy-done.57), kind=kCustom, calls=%fused_computation.2.clone | custom fusion | bytes 3149824 | tf_op jit(solution)/shard_map/jit(_take)/gather | solution.py:121
  278.8 44.0 %all-gather.15.cloned.1.call-done = bf16[768,2304]{1,0:T(8,128)(2,1)} async-done(((bf16[192,2304]{1,0:T(8,128)(2,1)}), bf16[768,2304]{1,0:T(8,128)(2,1)}) %all-gather.15.cloned.1.call-update) | async-done | bytes 3538960 | tf_op jit(solution)/shard_map/all_gather | solution.py:176
  333.3 23.6 %all-gather.17.cloned.1.call-done = bf16[1152,768]{1,0:T(8,128)(2,1)} async-done(((bf16[288,768]{1,0:T(8,128)(2,1)}), bf16[1152,768]{1,0:T(8,128)(2,1)}) %all-gather.17.cloned.1.call-update) | async-done | bytes 1769488 | tf_op jit(solution)/shard_map/all_gather | solution.py:177
  356.9 14.3 %fusion.42 = (f32[1024,1152]{1,0:T(8,128)}, f32[1024,1152]{1,0:T(8,128)S(1)}, f32[1024,1152]{1,0:T(8,128)S(1)}) fusion(f32[1024,2304]{1,0:T(8,128)} %fusion.93, bf16[1152,768]{1,0:T(8,128)(2,1)} %all-gather.17.cloned.1.call-done, bf16[1024,768]{0,1:T(8,128)(2,1)S(1)} %copy.75, pred[1024]{0:T(1024)(128)(4,1)S(1)} %copy-done.55, ...), kind=kOutput, calls=%fused_computation.111 | convolution fusion | flops 1890189312 | bytes 22218752 | tf_op jit(solution)/shard_map/td,fd->tf/dot_general | solution.py:249
  401.7 19.3 %multiply_reduce_fusion.1 = (f32[12,512]{1,0:T(8,128)S(1)}, f32[12,512,1024]{2,1,0:T(8,128)}) fusion(f32[12,512,1024]{2,1,0:T(8,128)} %get-tuple-element.103, f32[12,512]{1,0:T(8,128)S(1)} %get-tuple-element.102, bf16[512,12,64]{0,2,1:T(8,128)(2,1)S(1)} %bitcast.82, bf16[1024,12,64]{0,2,1:T(8,128)(2,1)S(1)} %bitcast.74), kind=kOutput, calls=%fused_computation.9 | convolution fusion | flops 824174592 | bytes 52740096 | tf_op jit(solution)/shard_map/qhd,khd->hqk/dot_general | solution.py:282
  421.0 19.1 %multiply_reduce_fusion = (f32[12,512]{1,0:T(8,128)S(1)}, f32[12,512,1024]{2,1,0:T(8,128)}) fusion(f32[12,512,1024]{2,1,0:T(8,128)} %get-tuple-element.101, f32[12,512]{1,0:T(8,128)S(1)} %get-tuple-element.100, bf16[512,12,64]{0,2,1:T(8,128)(2,1)S(1)} %bitcast.84, bf16[1024,12,64]{0,2,1:T(8,128)(2,1)S(1)} %bitcast.75), kind=kOutput, calls=%fused_computation.7 | convolution fusion | flops 824174592 | bytes 52740096 | tf_op jit(solution)/shard_map/qhd,khd->hqk/dot_general | solution.py:282
  440.2 17.0 %multiply_convert_fusion.1 = bf16[12,512,1024]{2,1,0:T(8,128)(2,1)S(1)} fusion(f32[12,512,1024]{2,1,0:T(8,128)} %get-tuple-element.111, f32[12,512]{1,0:T(8,128)S(1)} %get-tuple-element.110, f32[12,512,1024]{2,1,0:T(8,128)} %get-tuple-element.103, f32[12,512]{1,0:T(8,128)S(1)} %get-tuple-element.102), kind=kLoop, calls=%fused_computation.8 | loop fusion | flops 25165824 | bytes 62963712 | tf_op jit(solution)/shard_map/convert_element_type | solution.py:286
  457.3 26.9 %multiply_convert_fusion = bf16[12,512,1024]{2,1,0:T(8,128)(2,1)} fusion(f32[12,512,1024]{2,1,0:T(8,128)} %get-tuple-element.109, f32[12,512]{1,0:T(8,128)S(1)} %get-tuple-element.108, f32[12,512,1024]{2,1,0:T(8,128)} %get-tuple-element.101, f32[12,512]{1,0:T(8,128)S(1)} %get-tuple-element.100), kind=kLoop, calls=%fused_computation.6 | loop fusion | flops 25165824 | bytes 62963712 | tf_op jit(solution)/shard_map/convert_element_type | solution.py:286
  570.2 50.3 %reduce-scatter.5.cloned.1.call-done = bf16[192,2304]{1,0:T(8,128)(2,1)} async-done(((bf16[768,2304]{1,0:T(8,128)(2,1)}), bf16[192,2304]{1,0:T(8,128)(2,1)}) %reduce-scatter.5.cloned.1.call-update) | async-done | bytes 884752 | tf_op jit(solution)/shard_map/reduce_scatter | solution.py:335
  627.3 42.7 %all-gather.21.cloned.1.call-done = bf16[768,2304]{1,0:T(8,128)(2,1)} async-done(((bf16[192,2304]{1,0:T(8,128)(2,1)}), bf16[768,2304]{1,0:T(8,128)(2,1)}) %all-gather.21.cloned.1.call-update) | async-done | bytes 3538960 | tf_op jit(solution)/shard_map/all_gather | solution.py:240
  692.6 14.7 %all-reduce.10 = (bf16[192]{0:T(256)(128)(2,1)S(1)}, bf16[192]{0:T(256)(128)(2,1)S(1)}) all-reduce(bf16[192]{0:T(256)(128)(2,1)S(1)} %dynamic-slice.4, bf16[192]{0:T(256)(128)(2,1)S(1)} %dynamic-slice.6), channel_id=1, replica_groups=mesh['replica'=8,'group'=4] {'replica'}, use_global_device_ids=true, to_apply=%region_24.26 | all-reduce | flops 384 | bytes 1536 | tf_op jit(solution)/shard_map/psum | solution.py:352
  708.4 32.5 %all-reduce.16.cloned.1.call-done = (bf16[192,2304]{1,0:T(8,128)(2,1)}, bf16[192,768]{1,0:T(8,128)(2,1)}, bf16[192,2304]{1,0:T(8,128)(2,1)}, bf16[288,768]{1,0:T(8,128)(2,1)}) async-done(((bf16[192,2304]{1,0:T(8,128)(2,1)}, bf16[192,768]{1,0:T(8,128)(2,1)}, bf16[192,2304]{1,0:T(8,128)(2,1)}, bf16[288,768]{1,0:T(8,128)(2,1)}), (bf16[192,2304]{1,0:T(8,128)(2,1)}, bf16[192,768]{1,0:T(8,128)(2,1)}, ...) | async-done | bytes 2506768 | tf_op jit(solution)/shard_map/psum | solution.py:353
  747.6 111.1 %all-gather.23.cloned.1.call-done = bf16[8192,768]{0,1:T(8,128)(2,1)} async-done(((bf16[1024,768]{0,1:T(8,128)(2,1)}), bf16[8192,768]{0,1:T(8,128)(2,1)}) %all-gather.23.cloned.1.call-update) | async-done | bytes 12582928 | tf_op jit(solution)/shard_map/all_gather | solution.py:235
  858.7 16.6 %copy.73 = bf16[8192,768]{1,0:T(8,128)(2,1)} copy(bf16[8192,768]{0,1:T(8,128)(2,1)} %all-gather.23.cloned.1.call-done) | data formatting | bytes 25165824 | tf_op jit(solution)/shard_map/all_gather | solution.py:235
  886.9 88.9 %all-gather.25.cloned.1.call-done = bf16[8192,768]{0,1:T(8,128)(2,1)} async-done(((bf16[1024,768]{0,1:T(8,128)(2,1)}), bf16[8192,768]{0,1:T(8,128)(2,1)}) %all-gather.25.cloned.1.call-update) | async-done | bytes 12582928 | tf_op jit(solution)/shard_map/all_gather | solution.py:321
  975.8 16.7 %copy.76 = bf16[8192,768]{1,0:T(8,128)(2,1)} copy(bf16[8192,768]{0,1:T(8,128)(2,1)} %all-gather.25.cloned.1.call-done) | data formatting | bytes 25165824 | tf_op jit(solution)/shard_map/all_gather | solution.py:321
  992.5 11.8 %gather_fusion.3 = bf16[1024,768]{1,0:T(8,128)(2,1)} fusion(bf16[8192,768]{1,0:T(8,128)(2,1)} %copy.76, s32[1024]{0:T(1024)S(1)} %fusion.75), kind=kCustom, calls=%fused_computation.3.clone | custom fusion | bytes 3149824 | tf_op jit(solution)/shard_map/jit(_take)/gather | solution.py:121
  (273 shorter events, 289.4 us)
Async XLA Ops:
  7.2 121.9 %all-gather.11.cloned.1.call-start = ((), (), s32[]{:S(2)}) async-start(), calls=%async_computation.4 | async-start | bytes 14155776 | tf_op jit(solution)/shard_map/all_gather | solution.py:180
  7.9 239.7 %all-gather.19.cloned.1.call-start = ((), (), s32[]{:S(2)}) async-start(), calls=%async_computation.8 | async-start | bytes 14155776 | tf_op jit(solution)/shard_map/all_gather | solution.py:237
  8.7 264.7 %all-gather.13.cloned.1.call-start = ((), (), s32[]{:S(2)}) async-start(), calls=%async_computation.5 | async-start | bytes 1474560 | tf_op jit(solution)/shard_map/all_gather | solution.py:174
  9.5 313.3 %all-gather.15.cloned.1.call-start = ((), (), s32[]{:S(2)}) async-start(), calls=%async_computation.6 | async-start | bytes 4423680 | tf_op jit(solution)/shard_map/all_gather | solution.py:176
  10.6 346.4 %all-gather.17.cloned.1.call-start = ((), (), s32[]{:S(2)}) async-start(), calls=%async_computation.7 | async-start | bytes 2211840 | tf_op jit(solution)/shard_map/all_gather | solution.py:177
  13.4 53.8 %collective-permute-start.1 = (bf16[192,2304]{1,0:T(8,128)(2,1)}, bf16[192,2304]{1,0:T(8,128)(2,1)}, u32[]{:S(2)}, u32[]{:S(2)}) collective-permute-start(bf16[192,2304]{1,0:T(8,128)(2,1)} %get-tuple-element.67), channel_id=1, source_target_pairs={{0,3},{1,0},{2,1},{3,2},{4,7},{5,4},{6,5},{7,6},{8,11},{9,8},{10,9... | collective-permute-start | bytes 2654216 | tf_op jit(solution)/shard_map/ppermute | solution.py:32
  17.3 48.1 %collective-permute-start = (bf16[192,2304]{1,0:T(8,128)(2,1)}, bf16[192,2304]{1,0:T(8,128)(2,1)}, u32[]{:S(2)}, u32[]{:S(2)}) collective-permute-start(bf16[192,2304]{1,0:T(8,128)(2,1)} %get-tuple-element.67), channel_id=1, source_target_pairs={{0,1},{1,2},{2,3},{3,0},{4,5},{5,6},{6,7},{7,4},{8,9},{9,10},{10,1... | collective-permute-start | bytes 2654216 | tf_op jit(solution)/shard_map/ppermute | solution.py:27
  19.3 541.0 %reduce-scatter.7.cloned.1.call-start = ((), (), s32[]{:S(2)}) async-start(), calls=%async_computation.11 | async-start | bytes 1474560 | tf_op jit(solution)/shard_map/reduce_scatter | solution.py:338
  61.8 80.6 %copy-start.43 = (f32[768]{0:T(1024)}, f32[768]{0:T(1024)S(1)}, u32[]{:S(2)}) copy-start(f32[768]{0:T(1024)S(1)} %convert_element_type.173) | copy-start | bytes 9220
  65.4 21.3 %collective-permute-start.2 = (bf16[192,2304]{1,0:T(8,128)(2,1)}, bf16[192,2304]{1,0:T(8,128)(2,1)S(1)}, u32[]{:S(2)}, u32[]{:S(2)}) collective-permute-start(bf16[192,2304]{1,0:T(8,128)(2,1)} %collective-permute-done), channel_id=1, source_target_pairs={{0,1},{1,2},{2,3},{3,0},{4,5},{5,6},{6,7},{7,4},{8,9},{9,10},{10,1... | collective-permute-start | bytes 2654216 | tf_op jit(solution)/shard_map/ppermute | solution.py:27
  66.0 325.1 %copy-start.53 = (pred[1024]{0:T(1024)(128)(4,1)}, pred[1024]{0:T(1024)(128)(4,1)S(1)}, u32[]{:S(2)}) copy-start(pred[1024]{0:T(1024)(128)(4,1)S(1)} %get-tuple-element.86) | copy-start | bytes 3076
  86.8 42.3 %copy-start.22 = (bf16[768,2304]{1,0:T(8,128)(2,1)}, bf16[768,2304]{1,0:T(8,128)(2,1)S(1)}, u32[]{:S(2)}) copy-start(bf16[768,2304]{1,0:T(8,128)(2,1)S(1)} %constant_dynamic-update-slice_fusion) | copy-start | bytes 10616836
  141.3 132.1 %copy-start.1 = (bf16[1024,768]{0,1:T(8,128)(2,1)}, bf16[1024,768]{0,1:T(8,128)(2,1)S(1)}, u32[]{:S(2)}) copy-start(bf16[1024,768]{0,1:T(8,128)(2,1)S(1)} %copy.68) | copy-start | bytes 4718596
  191.3 33.6 %copy-start.25 = (bf16[1024,768]{0,1:T(8,128)(2,1)S(1)}, bf16[1024,768]{0,1:T(8,128)(2,1)}, u32[]{:S(2)}) copy-start(bf16[1024,768]{0,1:T(8,128)(2,1)} %copy.69) | copy-start | bytes 4718596
  261.2 95.8 %copy-start.5 = (bf16[1024,768]{0,1:T(8,128)(2,1)}, bf16[1024,768]{0,1:T(8,128)(2,1)S(1)}, u32[]{:S(2)}) copy-start(bf16[1024,768]{0,1:T(8,128)(2,1)S(1)} %copy.75) | copy-start | bytes 4718596
  276.8 46.0 %copy-start.58 = (f32[768]{0:T(1024)S(1)}, f32[768]{0:T(1024)}, u32[]{:S(2)}) copy-start(f32[768]{0:T(1024)} %convert_element_type.186) | copy-start | bytes 9220
  399.9 160.4 %reduce-scatter.11.cloned.1.call-start = ((), (), s32[]{:S(2)}) async-start(), calls=%async_computation.13 | async-start | bytes 2211840 | tf_op jit(solution)/shard_map/reduce_scatter | solution.py:347
  440.1 130.1 %reduce-scatter.9.cloned.1.call-start = ((), (), s32[]{:S(2)}) async-start(), calls=%async_computation.12 | async-start | bytes 4423680 | tf_op jit(solution)/shard_map/reduce_scatter | solution.py:344
  522.9 97.6 %reduce-scatter.5.cloned.1.call-start = ((), (), s32[]{:S(2)}) async-start(), calls=%async_computation.10 | async-start | bytes 4423680 | tf_op jit(solution)/shard_map/reduce_scatter | solution.py:335
  559.6 110.3 %all-gather.21.cloned.1.call-start = ((), (), s32[]{:S(2)}) async-start(), calls=%async_computation.9 | async-start | bytes 4423680 | tf_op jit(solution)/shard_map/all_gather | solution.py:240
  560.2 180.7 %all-reduce.16.cloned.1.call-start = ((), (), s32[]{:S(2)}) async-start(), calls=%async_computation.16 | async-start | bytes 5013504 | tf_op jit(solution)/shard_map/psum | solution.py:353
  620.6 238.1 %all-gather.23.cloned.1.call-start = ((), (), s32[]{:S(2)}) async-start(), calls=%async_computation.14 | async-start | bytes 14155776 | tf_op jit(solution)/shard_map/all_gather | solution.py:235
  627.2 49.8 %copy-start.50 = (f32[1024]{0:T(1024)S(1)}, f32[1024]{0:T(1024)}, u32[]{:S(2)}) copy-start(f32[1024]{0:T(1024)} %copy-done.49) | copy-start | bytes 12292
  627.2 348.6 %all-gather.25.cloned.1.call-start = ((), (), s32[]{:S(2)}) async-start(), calls=%async_computation.15 | async-start | bytes 14155776 | tf_op jit(solution)/shard_map/all_gather | solution.py:321
  (57 other events, 446.6 us)
Sparse Core Ops, SparseCore 0:
  9.6 119.4 all-gather.10
  130.7 114.8 all-gather.18
  247.5 25.7 all-gather.12
  275.6 47.1 all-gather.14
  324.4 32.4 all-gather.16
  400.0 28.6 reduce-scatter.6
  440.3 32.4 reduce-scatter.10
  523.1 47.1 reduce-scatter.8
  573.3 47.1 reduce-scatter.4
  622.8 47.1 all-gather.20
  672.6 68.2 all-reduce.15
  742.4 116.3 all-gather.22
  860.9 114.8 all-gather.24
